TPU v7x, 128 devices: a whole 4x4x4 slice. The times are simulated.
128 devices in a mesh: group: 8 (over z, core), pair: 16 (over y, x).
Axes of the slice: x: 4, y: 4, z: 4, core: 2. Of those that a mesh axis runs over, the one named last changes fastest.
Arguments:
- query_embed: bfloat16 [8, 16, 1024], P('group'), may hold values from -6 to 6
- teacher_scores: float32 [8, 16, 16, 32], P('group', 'pair'), may hold values from -9 to 9
- pair_owner: int32 [8, 16, 16, 32, 1], P('group', 'pair'), may hold values from 0 to 127; in each aligned block of 512 rows (0 to 511, 512 to 1023, ..., all dimensions but the last counted through in order) at most 8 rows name the same one
- pair_row: int32 [8, 16, 16, 32], P('group', 'pair'), may hold values from 0 to 2047
- passage_hidden: bfloat16 [262144, 1024], P(('group', 'pair')), may hold values from -24 to 24
- projection: bfloat16 [1024, 1024], replicated, may hold values from -0.1875 to 0.1875
Outputs:
- query_loss: float32 [8, 16], P('group', 'pair')
- query_grad: float32 [8, 16, 1024], P('group', 'pair')
- hidden_grad: bfloat16 [262144, 1024], P(('group', 'pair'))
- projection_grad: float32 [1024, 1024], P(('group', 'pair'))
Inputs may be any that keep to these rules, and one draw needn't show every extreme that they name: `pair_owner`: owners are numbered with group as the slower index. Among the 512 candidates held by one device, at most 8 name the same owner, and every draw has a device and an owner with exactly 8. `pair_row`: A passage may be named by several candidates.
All inputs are finite; a program needn't handle non-finite values.
Results may differ from a plain program's by a relative error of at most 0.022.
Values may be sent and summed in bfloat16 or wider, within the bound.
A program may use at most 128 MiB of HBM per device.

v0:
```python
import math
import jax
import jax.numpy as jnp
from jax import lax
from jax.sharding import PartitionSpec as P

loss_scale = 1024.0


def soft_steps(values_all, values_own):
    return jax.nn.sigmoid((values_all[:, None, :] - values_own[:, :, None]) * 2.0)


def score_slope(soft_step, grad_all, grad_own):
    slopes = soft_step * (1.0 - soft_step)
    return 2.0 * (jnp.sum(slopes * grad_all[:, None, :], -1) - grad_own * jnp.sum(slopes, -1))


def shards(query_embed, teacher_scores, pair_owner, pair_row, passage_hidden, projection):
    model_width = query_embed.shape[2]
    query_rows = query_embed.shape[1]
    cand_dev = teacher_scores.shape[3]
    pass_rows = passage_hidden.shape[0]
    pair_size = lax.axis_size("pair")
    group_size = lax.axis_size("group")
    devices = pair_size * group_size
    cand_all = cand_dev * pair_size
    pair_count = query_rows * cand_dev
    capacity = max(2, 2 * pair_count // devices)
    query_dev = query_rows // pair_size
    inv_root = 1.0 / math.sqrt(model_width)
    spearman_den = float(cand_all * (cand_all * cand_all - 1))
    embedded = jnp.dot(passage_hidden, projection, preferred_element_type=jnp.float32).astype(
        jnp.bfloat16
    )
    owner_dev = pair_owner.reshape(pair_count)
    row_index = pair_row.reshape(pair_count)
    owner_marks = (owner_dev[:, None] == jnp.arange(devices, dtype=jnp.int32)[None, :]).astype(
        jnp.int32
    )
    slot_index = jnp.sum(jnp.cumsum(owner_marks, axis=0) * owner_marks, axis=1) - 1
    requests = jnp.zeros((devices, capacity), jnp.int32).at[owner_dev, slot_index].set(row_index)
    queries = query_embed[0]
    asked_rows = lax.all_to_all(
        requests, ("group", "pair"), split_axis=0, concat_axis=0, tiled=True
    )
    vectors = jnp.take(embedded, asked_rows, axis=0)
    replies = lax.all_to_all(vectors, ("group", "pair"), split_axis=0, concat_axis=0, tiled=True)
    pair_vectors = replies[owner_dev, slot_index].reshape(query_rows, cand_dev, model_width)
    scores = (
        jnp.einsum("qd,qcd->qc", queries, pair_vectors, preferred_element_type=jnp.float32)
        * inv_root
    )
    teacher_own = teacher_scores.reshape(query_rows, cand_dev)
    scores_all, teacher_all = (
        lax.all_gather(scores, "pair", axis=1, tiled=True),
        lax.all_gather(teacher_own, "pair", axis=1, tiled=True),
    )
    soft_step = soft_steps(scores_all, scores)
    rank_student = 0.5 + jnp.sum(soft_step, -1)
    rank_teacher = 0.5 + jnp.sum(soft_steps(teacher_all, teacher_own), -1)
    rank_gap = rank_student - rank_teacher
    loss_part = 6.0 * jnp.sum(rank_gap * rank_gap, axis=1) / spearman_den
    rank_grad = loss_scale * 12.0 * rank_gap / spearman_den
    grad_all = lax.all_gather(rank_grad, "pair", axis=1, tiled=True)
    score_grad = score_slope(soft_step, grad_all, rank_grad)
    query_part = (
        jnp.sum(score_grad[:, :, None] * pair_vectors.astype(jnp.float32), axis=1) * inv_root
    )
    pair_grad = (
        score_grad[:, :, None] * queries.astype(jnp.float32)[:, None, :] * inv_root
    ).astype(jnp.bfloat16)
    query_sum, loss_own = (
        lax.psum_scatter(
            query_part.astype(jnp.bfloat16), "pair", scatter_dimension=0, tiled=True
        ).astype(jnp.float32),
        lax.psum_scatter(
            loss_part.astype(jnp.bfloat16), "pair", scatter_dimension=0, tiled=True
        ).astype(jnp.float32),
    )
    outgoing = (
        jnp.zeros((devices, capacity, model_width), jnp.bfloat16)
        .at[owner_dev, slot_index]
        .set(pair_grad.reshape(pair_count, model_width))
    )
    arrived = lax.all_to_all(outgoing, ("group", "pair"), split_axis=0, concat_axis=0, tiled=True)
    embed_grad = (
        jnp.zeros((pass_rows, model_width), jnp.float32)
        .at[asked_rows.reshape(-1)]
        .add(arrived.reshape(-1, model_width).astype(jnp.float32))
    )
    grad_rounded = embed_grad.astype(jnp.bfloat16)
    hidden_grad = jnp.einsum(
        "pe,de->pd", grad_rounded, projection, preferred_element_type=jnp.float32
    ).astype(jnp.bfloat16)
    projection_grad = lax.psum_scatter(
        jnp.einsum("pr,pe->re", passage_hidden, grad_rounded, preferred_element_type=jnp.float32),
        ("group", "pair"),
        scatter_dimension=0,
        tiled=True,
    )
    return (
        loss_own.reshape(1, query_dev),
        query_sum.reshape(1, query_dev, model_width),
        hidden_grad,
        projection_grad,
    )


def solution(mesh):
    placed = (
        P("group", None, None),
        P("group", "pair", None, None),
        P("group", "pair", None, None, None),
        P("group", "pair", None, None),
        P(("group", "pair"), None),
        P(),
    )
    return jax.shard_map(
        shards,
        mesh=mesh,
        in_specs=placed,
        out_specs=(
            P("group", "pair"),
            P("group", "pair", None),
            P(("group", "pair"), None),
            P(("group", "pair"), None),
        ),
        check_vma=False,
    )
```

profile of v0, /device:TPU:0, one launch (start us, length us, event | category | flops | bytes accessed | tf_op | source)
XLA Modules:
  0.0 964.4 jit_solution(8039499689911197415)
XLA Ops:
  7.2 0.0 copy-start
  7.2 0.9 eq.25
  8.1 0.8 eq.29
  8.9 0.8 reshape.243
  9.7 0.5 broadcast.268
  10.2 1.4 reduce.10
  11.5 0.1 reshape.209
  11.6 0.1 copy.29
  11.7 0.2 fusion.12
  12.0 0.2 fusion.11
  12.3 22.0 %scatter_fusion = s32[128,8]{0,1:T(8,128)S(1)} fusion(s32[128,8]{0,1:T(8,128)S(1)} %broadcast_in_dim.18, s32[512]{0:T(512)S(1)} %bitcast.82, s32[512]{0:T(512)S(1)} %reshape.243), kind=kCustom, calls=%fused_computation.2 | custom fusion | bytes 10240 | tf_op jit(solution)/shard_map/scatter | solution.py:42
  34.3 0.7 copy.31
  35.0 11.1 %all-to-all-start = ((s32[128,1,8]{2,1,0:T(1,128)}), s32[128,1,8]{2,1,0:T(1,128)S(1)}, u32[]{:S(2)}, u32[]{:S(2)}) async-start(s32[128,1,8]{2,1,0:T(1,128)} %copy.31), calls=%async_computation | async-start | bytes 131072 | tf_op jit(solution)/shard_map/all_to_all | solution.py:44
  46.2 0.0 copy-done
  46.2 8.3 convolution_convert_fusion.1
  54.5 1.2 all-to-all-done
  55.7 0.1 copy.33
  55.9 0.1 reshape.229
  56.0 8.8 gather_fusion
  64.7 0.0 copy-start.2
  64.7 0.0 copy-start.1
  64.7 3.2 bitcast_select_fusion
  67.9 9.1 all-to-all-start.1
  77.1 0.0 copy-done.2
  77.1 0.1 copy.35
  77.1 41.4 %all-gather = f32[1,1,16,512]{2,1,0,3:T(1,128)S(1)} all-gather(f32[1,1,16,32]{2,1,0,3:T(1,128)S(1)} %copy.35), channel_id=2, replica_groups=mesh['group'=8,'pair'=16] {'pair'}, dimensions={3}, use_global_device_ids=true | all-gather | bytes 34816 | tf_op jit(solution)/shard_map/all_gather | solution.py:57
  118.5 0.1 copy.36
  118.6 0.0 copy-done.1
  118.6 0.4 fusion.8
  119.1 0.0 all-to-all-done.1
  119.1 7.7 gather_fusion.1
  126.8 0.4 fusion.15
  127.2 22.0 %all-gather.1 = f32[16,32,16]{1,2,0:T(8,128)S(1)} all-gather(f32[1,32,16]{1,2,0:T(8,128)S(1)} %get-tuple-element.28), channel_id=1, replica_groups=mesh['group'=8,'pair'=16] {'pair'}, dimensions={0}, use_global_device_ids=true | all-gather | bytes 34816 | tf_op jit(solution)/shard_map/all_gather | solution.py:56
  149.3 0.1 reshape.264
  149.4 0.6 fusion.9
  149.9 22.6 %all-gather.2 = f32[16,32,16]{1,2,0:T(8,128)S(1)} all-gather(f32[1,32,16]{1,2,0:T(8,128)S(1)} %multiply_bitcast_fusion), channel_id=1, replica_groups=mesh['group'=8,'pair'=16] {'pair'}, dimensions={0}, use_global_device_ids=true | all-gather | bytes 34816 | tf_op jit(solution)/shard_map/all_gather | solution.py:65
  172.6 0.1 reshape.266
  172.7 0.5 multiply_reduce_fusion.1
  173.2 0.1 subtract_multiply_fusion.1
  173.3 0.1 reshape.226
  173.4 1.2 fusion.5
  174.7 1.6 broadcast_in_dim.23
  176.2 73.0 %scatter_fusion.1 = bf16[128,8,1024]{2,1,0:T(8,128)(2,1)} fusion(bf16[128,8,1024]{2,1,0:T(8,128)(2,1)} %broadcast_in_dim.23, s32[512]{0:T(512)S(1)} %bitcast.83, bf16[512,1024]{1,0:T(8,128)(2,1)} %fusion.5), kind=kCustom, calls=%fused_computation.3 | custom fusion | bytes 3149824 | tf_op jit(solution)/shard_map/scatter | solution.py:84
  249.2 8.3 all-to-all-start.2
  257.5 0.0 reduce-scatter.4.cloned.1.call-start
  257.6 0.8 reduce.11
  258.4 0.1 reshape.218
  258.5 28.3 %all-to-all-done.2 = bf16[128,8,1024]{2,1,0:T(8,128)(2,1)} async-done(((bf16[128,8,1024]{2,1,0:T(8,128)(2,1)}), bf16[128,8,1024]{2,1,0:T(8,128)(2,1)}, u32[]{:S(2)}, u32[]{:S(2)}) %all-to-all-start.2) | async-done | bytes 2097184 | tf_op jit(solution)/shard_map/all_to_all | solution.py:86
  286.8 13.4 %scatter_custom_fusion.2 = f32[2048,1024]{1,0:T(8,128)} fusion(s32[1024]{0:T(1024)S(1)} %bitcast.101, f32[]{:T(128)} %constant.26.clone.1, bf16[128,8,1024]{2,1,0:T(8,128)(2,1)} %all-to-all-done.2), kind=kCustom, calls=%fused_computation.5 | custom fusion | flops 2097152 | bytes 10485764 | tf_op jit(solution)/shard_map/scatter-add | solution.py:90
  300.2 11.2 %convolution_bitcast_fusion = f32[1024,1024]{0,1:T(8,128)} fusion(bf16[2048,1024]{1,0:T(8,128)(2,1)} %param.10, f32[2048,1024]{1,0:T(8,128)} %scatter_custom_fusion.2), kind=kOutput, calls=%fused_computation.10 | convolution fusion | flops 4297064448 | bytes 16777216 | tf_op jit(solution)/shard_map/pr,pe->re/dot_general | solution.py:97
  311.3 5.3 copy.41
  316.7 0.0 copy-start.3
  316.7 0.0 reduce-scatter.4.cloned.1.call-update
  316.7 0.5 multiply_reduce_fusion
  317.3 0.1 copy-done.3
  317.3 0.6 dynamic-slice
  317.9 72.1 %all-reduce.2 = (bf16[16]{0:T(256)(128)(2,1)S(1)}, bf16[16,1024]{1,0:T(8,128)(2,1)S(1)}) all-reduce(bf16[16]{0:T(256)(128)(2,1)S(1)} %multiply_convert_fusion.1, bf16[16,1024]{1,0:T(8,128)(2,1)S(1)} %multiply_convert_fusion), channel_id=3, replica_groups=mesh['group'=8,'pair'=16] {'pair'}, use_global_device_ids=true, to_apply=%region_7.8.clone | all-reduce | flops 16400 | bytes 65600
  390.0 1.2 dynamic-slice.1
  391.9 1.2 bitcast_convert_fusion.1
  393.2 9.5 convolution_convert_fusion
  402.6 553.7 %reduce-scatter.4.cloned.1.call-done = f32[8,1024]{1,0:T(8,128)} async-done(((f32[1024,1024]{1,0:T(8,128)}), f32[8,1024]{1,0:T(8,128)}) %reduce-scatter.4.cloned.1.call-update) | async-done | bytes 32784
  (21 shorter events, 0.3 us)
Async XLA Ops:
  7.2 39.0 %copy-start = (bf16[1024,1024]{1,0:T(8,128)(2,1)S(1)}, bf16[1024,1024]{1,0:T(8,128)(2,1)}, u32[]{:S(2)}) copy-start(bf16[1024,1024]{1,0:T(8,128)(2,1)} %param.11) | copy-start | bytes 6291460
  35.0 20.6 %all-to-all-start = ((s32[128,1,8]{2,1,0:T(1,128)}), s32[128,1,8]{2,1,0:T(1,128)S(1)}, u32[]{:S(2)}, u32[]{:S(2)}) async-start(s32[128,1,8]{2,1,0:T(1,128)} %copy.31), calls=%async_computation | async-start | bytes 131072 | tf_op jit(solution)/shard_map/all_to_all | solution.py:44
  64.7 12.3 %copy-start.2 = (f32[1,1,16,32]{3,2,1,0:T(8,128)S(1)}, f32[1,1,16,32]{3,2,1,0:T(8,128)}, u32[]{:S(2)}) copy-start(f32[1,1,16,32]{3,2,1,0:T(8,128)} %param.7) | copy-start | bytes 6148
  64.7 53.9 %copy-start.1 = (bf16[1,16,1024]{2,1,0:T(8,128)(2,1)S(1)}, bf16[1,16,1024]{2,1,0:T(8,128)(2,1)}, u32[]{:S(2)}) copy-start(bf16[1,16,1024]{2,1,0:T(8,128)(2,1)} %param.6) | copy-start | bytes 98308
  67.9 51.1 %all-to-all-start.1 = ((bf16[128,8,1024]{2,1,0:T(8,128)(2,1)}), bf16[128,8,1024]{2,1,0:T(8,128)(2,1)}, u32[]{:S(2)}, u32[]{:S(2)}) async-start(bf16[128,8,1024]{2,1,0:T(8,128)(2,1)} %bitcast_select_fusion), calls=%async_computation.1 | async-start | bytes 4194304 | tf_op jit(solution)/shard_map/all_to_all | solution.py:48
  249.2 37.6 %all-to-all-start.2 = ((bf16[128,8,1024]{2,1,0:T(8,128)(2,1)}), bf16[128,8,1024]{2,1,0:T(8,128)(2,1)}, u32[]{:S(2)}, u32[]{:S(2)}) async-start(bf16[128,8,1024]{2,1,0:T(8,128)(2,1)} %scatter_fusion.1), calls=%async_computation.2 | async-start | bytes 4194304 | tf_op jit(solution)/shard_map/all_to_all | solution.py:86
  257.5 698.9 %reduce-scatter.4.cloned.1.call-start = ((), (), s32[]{:S(2)}) async-start(), calls=%async_computation.4 | async-start | bytes 4227072
  316.7 0.7 copy-start.3
Sparse Core Ops, SparseCore 0:
  316.8 639.5 reduce-scatter.3
where the time goes:
time: 968 us; the launch traced here: 964 us
  waiting for transfers between devices  583 us (60%)
  blocking collectives  158 us (16%)
  local copies, waits for them, and re-layouts  125 us (13%)
  matrix products  29.3 us (3%)
  starting transfers between devices  28.6 us (3%)
  other arithmetic  24 us (2%)
  between operations  16.1 us (2%)
    unnamed x2, waiting for transfers between devices  554 us
    scatter x1, local copies, waits for them, and re-layouts, shards(): outgoing = jnp.zeros((devices, capacity, model_width), jnp.bfloat16).at[o...  73 us
    unnamed x1, blocking collectives  72.1 us
    all_gather x1, blocking collectives, shards(): lax.all_gather(teacher_own, 'pair', axis=1, tiled=True)  41.4 us
    all_to_all x1, waiting for transfers between devices, shards(): lax.all_to_all(outgoing, ('group', 'pair'), split_axis=0, concat_axis=0,...  28.3 us
    all_gather x1, blocking collectives, shards(): grad_all = lax.all_gather(rank_grad, 'pair', axis=1, tiled=True)  22.6 us
    all_gather x1, blocking collectives, shards(): lax.all_gather(scores, 'pair', axis=1, tiled=True)  22 us
    scatter x1, local copies, waits for them, and re-layouts, shards(): jnp.zeros((devices, capacity), jnp.int32).at[owner_dev, slot_index]  22 us
  transfers between devices with their start and end apart: 4, of which 3 were waited for; matrix products, arithmetic and copies ran while one was open for 2% of the time, Pallas kernels for 0%

commit v1 on v0

--- a/solution.py
+++ b/solution.py
@@ -53,7 +53,9 @@
     )
     teacher_own = teacher_scores.reshape(query_rows, cand_dev)
     scores_all, teacher_all = (
-        lax.all_gather(scores, "pair", axis=1, tiled=True),
+        jnp.concatenate(
+            lax.all_to_all(jnp.stack([scores] * lax.axis_size("pair")), "pair", 0, 0), axis=1
+        ),
         lax.all_gather(teacher_own, "pair", axis=1, tiled=True),
     )
     soft_step = soft_steps(scores_all, scores)

time: 968 us -> 966 us (level)
    all_to_all x0 -> x1, blocking collectives: none -> 38.2 us  [shards(): lax.all_to_all(vectors, ('group', 'pair'), split_axis=0, concat_axis=0, t...]
    all_gather x1 -> x0, blocking collectives: 22 us -> none  [shards(): lax.all_gather(scores, 'pair', axis=1, tiled=True)]
    all_gather x1, blocking collectives: 41.4 us -> 24 us  [shards(): lax.all_gather(teacher_own, 'pair', axis=1, tiled=True)]
where the time goes in v1:
time: 966 us; the launch traced here: 962 us
  waiting for transfers between devices  583 us (60%)
  blocking collectives  157 us (16%)
  local copies, waits for them, and re-layouts  128 us (13%)
  matrix products  29.3 us (3%)
  other arithmetic  26.2 us (3%)
  starting transfers between devices  21.5 us (2%)
  between operations  16.1 us (2%)
    unnamed x2, waiting for transfers between devices  554 us
    scatter x1, local copies, waits for them, and re-layouts, shards(): outgoing = jnp.zeros((devices, capacity, model_width), jnp.bfloat16).at[o...  73 us
    unnamed x1, blocking collectives  72.1 us
    all_to_all x1, blocking collectives, shards(): lax.all_to_all(vectors, ('group', 'pair'), split_axis=0, concat_axis=0, t...  38.2 us
    all_to_all x1, waiting for transfers between devices, shards(): lax.all_to_all(outgoing, ('group', 'pair'), split_axis=0, concat_axis=0,...  28.3 us
    all_gather x1, blocking collectives, shards(): lax.all_gather(teacher_own, 'pair', axis=1, tiled=True)  24 us
    all_gather x1, blocking collectives, shards(): grad_all = lax.all_gather(rank_grad, 'pair', axis=1, tiled=True)  23.1 us
    scatter x1, local copies, waits for them, and re-layouts, shards(): jnp.zeros((devices, capacity), jnp.int32).at[owner_dev, slot_index]  22 us
  transfers between devices with their start and end apart: 4, of which 3 were waited for; matrix products, arithmetic and copies ran while one was open for 2% of the time, Pallas kernels for 0%

profile of v1, /device:TPU:0, one launch (start us, length us, event | category | flops | bytes accessed | tf_op | source)
XLA Modules:
  0.0 962.0 jit_solution(1709333063075192004)
XLA Ops:
  7.2 0.0 copy-start
  7.2 0.9 eq.25
  8.1 0.8 eq.29
  8.9 0.8 reshape.249
  9.7 0.5 broadcast.269
  10.2 1.4 reduce.10
  11.5 0.1 reshape.214
  11.6 0.1 copy.38
  11.7 0.2 fusion.12
  12.0 0.2 fusion.11
  12.3 22.0 %scatter_fusion = s32[128,8]{0,1:T(8,128)S(1)} fusion(s32[128,8]{0,1:T(8,128)S(1)} %broadcast_in_dim.18, s32[512]{0:T(512)S(1)} %bitcast.76, s32[512]{0:T(512)S(1)} %reshape.249), kind=kCustom, calls=%fused_computation.2 | custom fusion | bytes 10240 | tf_op jit(solution)/shard_map/scatter | solution.py:42
  34.3 0.7 copy.40
  35.0 11.1 %all-to-all-start = ((s32[128,1,8]{2,1,0:T(1,128)}), s32[128,1,8]{2,1,0:T(1,128)S(1)}, u32[]{:S(2)}, u32[]{:S(2)}) async-start(s32[128,1,8]{2,1,0:T(1,128)} %copy.40), calls=%async_computation | async-start | bytes 131072 | tf_op jit(solution)/shard_map/all_to_all | solution.py:44
  46.2 0.0 copy-done
  46.2 8.3 convolution_convert_fusion.1
  54.4 1.2 all-to-all-done
  55.7 0.1 copy.42
  55.9 0.1 reshape.235
  56.0 8.8 gather_fusion
  64.7 1.9 bitcast_select_fusion
  66.6 38.2 %all_to_all.30 = bf16[128,8,1024]{2,1,0:T(8,128)(2,1)} all-to-all(bf16[128,8,1024]{2,1,0:T(8,128)(2,1)S(1)} %bitcast_select_fusion), channel_id=1, replica_groups=mesh['group'=8,'pair'=16] {'group','pair'}, dimensions={0} | all-to-all | bytes 4194304 | tf_op jit(solution)/shard_map/all_to_all | solution.py:48
  104.8 7.7 gather_fusion.1
  112.5 0.0 copy-done.1
  112.5 0.4 fusion.15
  112.9 0.7 reshape.301
  113.7 4.2 all-to-all-start.2
  117.8 0.0 copy-done.5
  117.9 0.7 copy.44
  118.5 24.0 %all-gather = f32[1,1,16,512]{2,1,0,3:T(1,128)S(1)} all-gather(f32[1,1,16,32]{2,1,0,3:T(1,128)} %copy.44), channel_id=2, replica_groups=mesh['group'=8,'pair'=16] {'pair'}, dimensions={3}, use_global_device_ids=true | all-gather | bytes 34816 | tf_op jit(solution)/shard_map/all_gather | solution.py:59
  142.6 0.7 copy.45
  143.3 0.0 all-to-all-done.2
  143.3 0.5 broadcast.276
  143.8 1.5 reduce.12
  145.3 0.1 reshape.302
  145.4 0.1 sub.58
  145.5 1.5 fusion.8
  147.1 0.0 copy-start.3
  147.1 0.6 copy-done.3
  147.7 0.0 copy-done.4
  147.7 23.1 %all-gather.1 = f32[16,32,16]{1,2,0:T(8,128)S(1)} all-gather(f32[1,32,16]{1,2,0:T(8,128)S(1)} %multiply_bitcast_fusion), channel_id=1, replica_groups=mesh['group'=8,'pair'=16] {'pair'}, dimensions={0}, use_global_device_ids=true | all-gather | bytes 34816 | tf_op jit(solution)/shard_map/all_gather | solution.py:67
  170.9 0.1 reshape.270
  171.0 1.4 fusion.9
  172.3 0.8 subtract_multiply_fusion.1
  173.2 0.1 reshape.232
  173.2 1.2 fusion.5
  174.5 1.6 broadcast_in_dim.40
  176.0 73.0 %scatter_fusion.1 = bf16[128,8,1024]{2,1,0:T(8,128)(2,1)} fusion(bf16[128,8,1024]{2,1,0:T(8,128)(2,1)} %broadcast_in_dim.40, s32[512]{0:T(512)S(1)} %bitcast.77, bf16[512,1024]{1,0:T(8,128)(2,1)} %fusion.5), kind=kCustom, calls=%fused_computation.3 | custom fusion | bytes 3149824 | tf_op jit(solution)/shard_map/scatter | solution.py:86
  249.0 6.2 all-to-all-start.3
  255.2 0.0 reduce-scatter.4.cloned.1.call-start
  255.3 0.8 reduce.11
  256.1 0.1 reshape.224
  256.2 28.3 %all-to-all-done.3 = bf16[128,8,1024]{2,1,0:T(8,128)(2,1)} async-done(((bf16[128,8,1024]{2,1,0:T(8,128)(2,1)}), bf16[128,8,1024]{2,1,0:T(8,128)(2,1)}, u32[]{:S(2)}, u32[]{:S(2)}) %all-to-all-start.3) | async-done | bytes 2097184 | tf_op jit(solution)/shard_map/all_to_all | solution.py:88
  284.5 13.4 %scatter_custom_fusion.2 = f32[2048,1024]{1,0:T(8,128)} fusion(s32[1024]{0:T(1024)S(1)} %bitcast.94, f32[]{:T(128)} %constant.26.clone.1, bf16[128,8,1024]{2,1,0:T(8,128)(2,1)} %all-to-all-done.3), kind=kCustom, calls=%fused_computation.5 | custom fusion | flops 2097152 | bytes 10485764 | tf_op jit(solution)/shard_map/scatter-add | solution.py:92
  297.9 11.2 %convolution_bitcast_fusion = f32[1024,1024]{0,1:T(8,128)} fusion(bf16[2048,1024]{1,0:T(8,128)(2,1)} %param.10, f32[2048,1024]{1,0:T(8,128)} %scatter_custom_fusion.2), kind=kOutput, calls=%fused_computation.10 | convolution fusion | flops 4297064448 | bytes 16777216 | tf_op jit(solution)/shard_map/pr,pe->re/dot_general | solution.py:99
  309.0 5.3 copy.50
  314.4 0.0 reduce-scatter.4.cloned.1.call-update
  314.4 0.5 multiply_reduce_fusion
  315.0 0.1 copy-done.6
  315.0 0.6 dynamic-slice
  315.6 72.1 %all-reduce.2 = (bf16[16]{0:T(256)(128)(2,1)S(1)}, bf16[16,1024]{1,0:T(8,128)(2,1)S(1)}) all-reduce(bf16[16]{0:T(256)(128)(2,1)S(1)} %multiply_convert_fusion.1, bf16[16,1024]{1,0:T(8,128)(2,1)S(1)} %multiply_convert_fusion), channel_id=3, replica_groups=mesh['group'=8,'pair'=16] {'pair'}, use_global_device_ids=true, to_apply=%region_7.8.clone | all-reduce | flops 16400 | bytes 65600
  387.7 1.2 dynamic-slice.1
  389.6 1.2 bitcast_convert_fusion.1
  390.8 9.5 convolution_convert_fusion
  400.3 553.7 %reduce-scatter.4.cloned.1.call-done = f32[8,1024]{1,0:T(8,128)} async-done(((f32[1024,1024]{1,0:T(8,128)}), f32[8,1024]{1,0:T(8,128)}) %reduce-scatter.4.cloned.1.call-update) | async-done | bytes 32784
  (28 shorter events, 0.4 us)
Async XLA Ops:
  7.2 39.0 %copy-start = (bf16[1024,1024]{1,0:T(8,128)(2,1)S(1)}, bf16[1024,1024]{1,0:T(8,128)(2,1)}, u32[]{:S(2)}) copy-start(bf16[1024,1024]{1,0:T(8,128)(2,1)} %param.11) | copy-start | bytes 6291460
  35.0 20.6 %all-to-all-start = ((s32[128,1,8]{2,1,0:T(1,128)}), s32[128,1,8]{2,1,0:T(1,128)S(1)}, u32[]{:S(2)}, u32[]{:S(2)}) async-start(s32[128,1,8]{2,1,0:T(1,128)} %copy.40), calls=%async_computation | async-start | bytes 131072 | tf_op jit(solution)/shard_map/all_to_all | solution.py:44
  104.8 7.7 copy-start.1
  104.8 13.1 %copy-start.5 = (f32[1,1,16,32]{3,2,1,0:T(8,128)S(1)}, f32[1,1,16,32]{3,2,1,0:T(8,128)}, u32[]{:S(2)}) copy-start(f32[1,1,16,32]{3,2,1,0:T(8,128)} %param.7) | copy-start | bytes 6148
  113.7 29.6 %all-to-all-start.2 = ((f32[16,1,512]{2,1,0:T(1,128)}), f32[16,1,512]{2,1,0:T(1,128)}, u32[]{:S(2)}, u32[]{:S(2)}) async-start(f32[16,1,512]{2,1,0:T(1,128)} %reshape.301), calls=%async_computation.2 | async-start | bytes 65536 | tf_op jit(solution)/shard_map/all_to_all | solution.py:57
  145.5 1.6 copy-start.2
  147.1 0.6 copy-start.3
  147.1 0.6 copy-start.4
  249.0 35.5 %all-to-all-start.3 = ((bf16[128,8,1024]{2,1,0:T(8,128)(2,1)}), bf16[128,8,1024]{2,1,0:T(8,128)(2,1)}, u32[]{:S(2)}, u32[]{:S(2)}) async-start(bf16[128,8,1024]{2,1,0:T(8,128)(2,1)} %scatter_fusion.1), calls=%async_computation.3 | async-start | bytes 4194304 | tf_op jit(solution)/shard_map/all_to_all | solution.py:88
  255.2 698.8 %reduce-scatter.4.cloned.1.call-start = ((), (), s32[]{:S(2)}) async-start(), calls=%async_computation.5 | async-start | bytes 4227072
  314.4 0.7 copy-start.6
Sparse Core Ops, SparseCore 0:
  314.5 639.4 reduce-scatter.3
